TPU v7x, 32 devices: a whole 2x2x4 slice. The times are simulated.
32 devices in a mesh: rep: 2 (over y), tm: 8 (over z, x), col: 2 (over core).
Axes of the slice: x: 2, y: 2, z: 4, core: 2. Of those that a mesh axis runs over, the one named last changes fastest.
Arguments:
- diagonal_block_inverse: float32 [32, 512, 512], P(('rep', 'tm'), None, 'col'), parts along dimension 0, may hold values from -0.1 to 4.5, as said below
- step_map: bfloat16 [32, 512, 512], P(('rep', 'tm'), None, 'col'), parts along dimension 0, may hold values from -1.1 to 1.1
- arrow_map: bfloat16 [32, 32, 512], P(('rep', 'tm'), None, 'col'), parts along dimension 0, may hold values from -0.1796875 to 0.1796875
- arrow_cov: float32 [64, 32], P('rep'), parts along dimension 0, may hold values from -0.5 to 2.5, as said below
Outputs:
- blocks: float32 [32, 512, 512], P(('rep', 'tm'), None, 'col'), parts along dimension 0
- cross: float32 [32, 32, 512], P(('rep', 'tm'), None, 'col'), parts along dimension 0
There are 2 independent parts, one for each index of `rep`. A program takes and returns all parts, laid end to end along the dimension named above; each array names one. Nothing has to cross between parts.
Inputs may be any that keep to these rules, and one draw needn't show every extreme that they name: `diagonal_block_inverse`: symmetric in its last two dimensions. `arrow_cov`: symmetric.
All inputs are finite; a program needn't handle non-finite values.
Results may differ from a plain program's by a relative error of at most 0.019.
Values may be sent and summed in bfloat16 or wider, within the bound.
A program may use at most 384 MiB of HBM per device.

v0:
```python
import jax
import jax.numpy as jnp
from jax import lax
from jax.sharding import PartitionSpec as P


def prefix(x, axis, join, neutral):
    count = lax.axis_size(axis)
    place = lax.axis_index(axis)
    ahead = count - 1 - place
    gathered = jax.tree.map(
        lambda a, kind: lax.all_gather(a.astype(kind), axis),
        x,
        jax.tree.map(lambda a: jnp.bfloat16 if a.dtype == jnp.float32 else a.dtype, x),
    )
    state = jax.tree.map(lambda a, e: jnp.zeros_like(a) + jnp.asarray(e, a.dtype), x, neutral)

    def one(turn, state):
        source = count - 1 - turn
        return join(
            state,
            jax.tree.map(
                lambda a, own: lax.dynamic_index_in_dim(a, source, 0, False).astype(own.dtype),
                gathered,
                x,
            ),
        )

    return lax.fori_loop(0, ahead, one, state)


def product(left, right):
    return jnp.dot(
        left.astype(jnp.bfloat16), right.astype(jnp.bfloat16), preferred_element_type=jnp.float32
    )


def compose(earlier, later):
    early_p, early_q, early_g, early_h, early_s = earlier
    late_p, late_q, late_g, late_h, late_s = later
    pushed = product(early_p, late_g) + product(early_q.T, late_h)
    cross_g = product(early_q, late_g)
    joined_p = late_p + product(late_g.T, pushed) + product(late_h.T, cross_g)
    joined_q = late_q + late_s * cross_g
    joined_g = product(early_g, late_g)
    joined_h = product(early_h, late_g) + early_s * late_h
    return (joined_p, joined_q, joined_g, joined_h, early_s * late_s)


def single_map(diag_block, coupling, arrow_rows):
    return (
        diag_block,
        jnp.zeros(arrow_rows.shape, jnp.float32),
        coupling.astype(jnp.float32),
        arrow_rows.astype(jnp.float32),
        jnp.float32(-1.0),
    )


def local_composite(diag_full, coupling_full, arrow_full):
    count = diag_full.shape[0]
    mapping = single_map(diag_full[count - 1], coupling_full[count - 1], arrow_full[count - 1])
    mapping = compose(mapping, single_map(diag_full[0], coupling_full[0], arrow_full[0]))
    return mapping


def neutral(nodes, effects):
    return (
        jnp.zeros((nodes, nodes), jnp.float32),
        jnp.zeros((effects, nodes), jnp.float32),
        jnp.eye(nodes, dtype=jnp.float32),
        jnp.zeros((effects, nodes), jnp.float32),
        jnp.float32(1.0),
    )


def entry_state(mapping, arrow_cov):
    joined_p, joined_q, joined_g, joined_h, joined_s = mapping
    weighted = product(arrow_cov, joined_h)
    return (joined_p + product(joined_h.T, weighted), joined_q + joined_s * weighted)


def advance(diag_cols, coupling, arrow_rows, current, cross, arrow_cov, start, span_cols):
    lower = product(cross, coupling) + product(arrow_cov, arrow_rows)
    coupling_cols = lax.dynamic_slice_in_dim(coupling, start, span_cols, 1)
    arrow_cols = lax.dynamic_slice_in_dim(arrow_rows, start, span_cols, 1)
    lower_cols = lax.dynamic_slice_in_dim(lower, start, span_cols, 1)
    upper = product(current, coupling_cols) + product(cross.T, arrow_cols)
    fresh_cols = diag_cols + product(coupling.T, upper) + product(arrow_rows.T, lower_cols)
    return (fresh_cols, -lower)


def shards(diagonal_block_inverse, step_map, arrow_map, arrow_cov):
    span_cols = diagonal_block_inverse.shape[2]
    diag_full = lax.all_gather(
        diagonal_block_inverse.astype(jnp.bfloat16), "col", axis=2, tiled=True
    ).astype(diagonal_block_inverse.dtype)
    coupling_full, arrow_full = (
        lax.all_gather(step_map, "col", axis=2, tiled=True),
        lax.all_gather(arrow_map, "col", axis=2, tiled=True),
    )
    nodes = coupling_full.shape[1]
    effects = arrow_full.shape[1]
    count = diag_full.shape[0]
    composite = local_composite(diag_full, coupling_full, arrow_full)
    above = prefix(composite, "tm", compose, neutral(nodes, effects))
    current, cross = entry_state(above, arrow_cov)
    start = lax.axis_index("col") * span_cols
    blocks_out = []
    cross_out = []
    for position in range(count - 1, -1, -1):
        fresh_cols, cross = advance(
            diagonal_block_inverse[position],
            coupling_full[position],
            arrow_full[position],
            current,
            cross,
            arrow_cov,
            start,
            span_cols,
        )
        if position > 0:
            current = lax.all_gather(fresh_cols.astype(jnp.bfloat16), "col", axis=1, tiled=True)
        blocks_out.append(fresh_cols)
        cross_out.append(lax.dynamic_slice_in_dim(cross, start, span_cols, 1))
    return (jnp.stack(blocks_out[::-1]), jnp.stack(cross_out[::-1]))


def solution(mesh):
    return jax.shard_map(
        shards,
        mesh=mesh,
        in_specs=(
            P(("rep", "tm"), None, "col"),
            P(("rep", "tm"), None, "col"),
            P(("rep", "tm"), None, "col"),
            P("rep", None),
        ),
        out_specs=(P(("rep", "tm"), None, "col"), P(("rep", "tm"), None, "col")),
        check_vma=False,
    )
```

profile of v0, /device:TPU:0, one launch (start us, length us, event | category | flops | bytes accessed | tf_op | source)
XLA Modules:
  0.0 276.5 jit_solution(14894213775358241003)
XLA Ops:
  8.0 1.6 copy.6
  10.6 2.0 all_gather.41
  12.5 8.8 %all-gather.11.cloned.1.call-done = bf16[2,512,512]{2,1,0:T(8,128)(2,1)} async-done(((bf16[2,512,256]{2,1,0:T(8,128)(2,1)}), bf16[2,512,512]{2,1,0:T(8,128)(2,1)}) %all-gather.11.cloned.1.call-update) | async-done | bytes 1048592 | tf_op jit(solution)/shard_map/all_gather | solution.py:99
  21.3 1.3 multiply_convert_fusion
  22.6 10.5 %all-gather.9.cloned.1.call-done = bf16[2,512,512]{1,2,0:T(8,128)(2,1)} async-done(((bf16[2,512,256]{1,2,0:T(8,128)(2,1)}), bf16[2,512,512]{1,2,0:T(8,128)(2,1)}) %all-gather.9.cloned.1.call-update) | async-done | bytes 1048592 | tf_op jit(solution)/shard_map/all_gather | solution.py:95
  33.1 1.7 fusion.44
  34.8 1.8 fusion.31
  37.8 1.2 convolution_convert_fusion
  40.5 21.7 %all-reduce = bf16[8]{0:T(256)(128)(2,1)S(1)} all-reduce(bf16[8]{0:T(256)(128)(2,1)S(1)} %dynamic-update-slice), channel_id=1, replica_groups=mesh['rep'=2,'tm'=8,'col'=2] {'tm'}, use_global_device_ids=true, to_apply=%add | all-reduce | flops 8 | bytes 32
  63.0 31.5 %all-gather.2 = bf16[256,512]{1,0:T(8,128)(2,1)S(1)} all-gather(bf16[32,512]{1,0:T(8,128)(2,1)S(1)} %fusion.43), channel_id=4, replica_groups=mesh['rep'=2,'tm'=8,'col'=2] {'tm'}, dimensions={0}, use_global_device_ids=true | all-gather | bytes 294912 | tf_op jit(solution)/shard_map/all_gather | solution.py:12
  94.5 33.4 %all-gather.3 = bf16[256,512]{1,0:T(8,128)(2,1)} all-gather(bf16[32,512]{1,0:T(8,128)(2,1)S(1)} %get-tuple-element.218), channel_id=5, replica_groups=mesh['rep'=2,'tm'=8,'col'=2] {'tm'}, dimensions={0}, use_global_device_ids=true | all-gather | bytes 294912 | tf_op jit(solution)/shard_map/all_gather | solution.py:12
  129.0 6.6 %copy.11 = bf16[4096,512]{1,0:T(8,128)(2,1)} copy(bf16[4096,512]{0,1:T(8,128)(2,1)} %all-gather.13.cloned.1.call-done) | data formatting | bytes 8388608 | tf_op jit(solution)/shard_map/while | solution.py:29
  135.6 58.4 %all-gather.15.cloned.1.call-done = bf16[4096,512]{1,0:T(8,128)(2,1)} async-done(((bf16[512,512]{1,0:T(8,128)(2,1)}), bf16[4096,512]{1,0:T(8,128)(2,1)}) %all-gather.15.cloned.1.call-update) | async-done | bytes 4194320 | tf_op jit(solution)/shard_map/all_gather | solution.py:12
  194.1 58.9 %while.20 = (s32[]{:T(128)}, f32[512,512]{1,0:T(8,128)S(1)}, f32[32,512]{1,0:T(8,128)S(1)}, bf16[32,512]{1,0:T(8,128)(2,1)S(1)}, f32[]{:T(128)}, /*index=5*/s32[...) while((s32[]{:T(128)}, f32[512,512]{1,0:T(8,128)S(1)}, ...), condition=%wide.region_1.2_spmd, body=%wide.region_0.1_spmd.sunk | while | flops 605716480 | bytes 9573083 | solution.py:29
  194.1 1.5 fusion.161
  195.6 1.9 convolution_add_fusion.12
  198.9 1.2 convert_add_fusion.2
  200.5 1.2 fusion.162
  202.5 1.5 fusion.161
  204.0 1.9 convolution_add_fusion.12
  207.3 1.2 convert_add_fusion.2
  208.9 1.2 fusion.162
  210.9 1.5 fusion.161
  212.5 1.9 convolution_add_fusion.12
  215.8 1.2 convert_add_fusion.2
  217.4 1.2 fusion.162
  219.3 1.5 fusion.161
  220.9 1.9 convolution_add_fusion.12
  224.2 1.2 convert_add_fusion.2
  225.8 1.2 fusion.162
  227.7 1.5 fusion.161
  229.3 1.9 convolution_add_fusion.12
  232.6 1.2 convert_add_fusion.2
  234.2 1.2 fusion.162
  236.2 1.5 fusion.161
  237.7 1.9 convolution_add_fusion.12
  241.0 1.2 convert_add_fusion.2
  242.6 1.2 fusion.162
  244.6 1.5 fusion.161
  246.1 1.9 convolution_add_fusion.12
  249.4 1.2 convert_add_fusion.2
  251.0 1.2 fusion.162
  253.1 1.3 fusion.45
  257.6 2.2 fusion.40
  259.8 1.7 fusion.38
  262.5 2.2 all_gather.51
  264.7 1.3 fusion.58
  268.0 1.3 copy.10
  (79 shorter events, 20.2 us)
Async XLA Ops:
  7.2 3.4 %copy-start.8 = (bf16[2,32,256]{2,1,0:T(8,128)(2,1)S(1)}, bf16[2,32,256]{2,1,0:T(8,128)(2,1)}, u32[]{:S(2)}) copy-start(bf16[2,32,256]{2,1,0:T(8,128)(2,1)} %param.8) | copy-start | bytes 98308
  7.2 14.1 %all-gather.11.cloned.1.call-start = ((), (), s32[]{:S(2)}) async-start(), calls=%async_computation.1 | async-start | bytes 1572864 | tf_op jit(solution)/shard_map/all_gather | solution.py:99
  7.9 25.2 %all-gather.9.cloned.1.call-start = ((), (), s32[]{:S(2)}) async-start(), calls=%async_computation | async-start | bytes 1572864 | tf_op jit(solution)/shard_map/all_gather | solution.py:95
  9.5 3.0 %copy-start.2 = (f32[2,512,256]{1,2,0:T(8,128)}, f32[2,512,256]{1,2,0:T(8,128)S(1)}, u32[]{:S(2)}) copy-start(f32[2,512,256]{1,2,0:T(8,128)S(1)} %copy.6) | copy-start | bytes 3145732
  10.5 118.5 %all-gather.13.cloned.1.call-start = ((), (), s32[]{:S(2)}) async-start(), calls=%async_computation.2 | async-start | bytes 4718592 | tf_op jit(solution)/shard_map/all_gather | solution.py:12
  12.5 50.3 %copy-start.4 = (bf16[2,32,512]{2,1,0:T(8,128)(2,1)}, bf16[2,32,512]{2,1,0:T(8,128)(2,1)S(1)}, u32[]{:S(2)}) copy-start(bf16[2,32,512]{2,1,0:T(8,128)(2,1)S(1)} %all_gather.41) | copy-start | bytes 196612
  21.3 16.5 %copy-start = (bf16[2,512,512]{2,1,0:T(8,128)(2,1)S(1)}, bf16[2,512,512]{2,1,0:T(8,128)(2,1)}, u32[]{:S(2)}) copy-start(bf16[2,512,512]{2,1,0:T(8,128)(2,1)} %all-gather.11.cloned.1.call-done) | copy-start | bytes 3145732
  34.7 4.3 %copy-start.9 = (u32[32]{0:T(128)S(1)}, u32[32]{0:T(128)}, u32[]{:S(2)}) copy-start(u32[32]{0:T(128)} %constant.77) | copy-start | bytes 388
  37.8 156.2 %all-gather.15.cloned.1.call-start = ((), (), s32[]{:S(2)}) async-start(), calls=%async_computation.3 | async-start | bytes 4718592 | tf_op jit(solution)/shard_map/all_gather | solution.py:12
  194.1 59.0 %copy-start.6 = (f32[32,32]{1,0:T(8,128)S(1)}, f32[32,32]{1,0:T(8,128)}, u32[]{:S(2)}) copy-start(f32[32,32]{1,0:T(8,128)} %param.9) | copy-start | bytes 12292
  253.0 6.8 %copy-start.1 = (bf16[2,512,512]{2,1,0:T(8,128)(2,1)S(1)}, bf16[2,512,512]{2,1,0:T(8,128)(2,1)}, u32[]{:S(2)}) copy-start(bf16[2,512,512]{2,1,0:T(8,128)(2,1)} %all-gather.11.cloned.1.call-done) | copy-start | bytes 3145732
  253.0 6.8 %copy-start.3 = (f32[2,512,256]{1,2,0:T(8,128)S(1)}, f32[2,512,256]{1,2,0:T(8,128)}, u32[]{:S(2)}) copy-start(f32[2,512,256]{1,2,0:T(8,128)} %copy-done.2) | copy-start | bytes 3145732
  253.0 8.5 %copy-start.5 = (bf16[2,32,512]{2,1,0:T(8,128)(2,1)S(1)}, bf16[2,32,512]{2,1,0:T(8,128)(2,1)}, u32[]{:S(2)}) copy-start(bf16[2,32,512]{2,1,0:T(8,128)(2,1)} %copy-done.4) | copy-start | bytes 196612
  255.4 10.6 %copy-start.7 = (bf16[1,32,512]{2,1,0:T(8,128)(2,1)S(1)}, bf16[1,32,512]{2,1,0:T(8,128)(2,1)}, u32[]{:S(2)}) copy-start(bf16[1,32,512]{2,1,0:T(8,128)(2,1)} %get-tuple-element.216) | copy-start | bytes 98308
Sparse Core Ops, SparseCore 0:
  9.5 11.6 all-gather.10
  22.8 10.2 all-gather.8
  37.9 81.8 all-gather.12
  121.7 72.1 all-gather.14
where the time goes:
time: 278 us; the launch traced here: 276 us
  blocking collectives  90.7 us (33%)
  waiting for transfers between devices  78.3 us (28%)
  matrix products  62.8 us (23%)
  local copies, waits for them, and re-layouts  17.5 us (6%)
  between operations  14 us (5%)
  loops' own time  10.3 us (4%)
    all_gather x2, blocking collectives, prefix(): lax.all_gather(a.astype(kind), axis)  64.9 us
    dot_general x52, matrix products, product(): jnp.dot(left.astype(jnp.bfloat16), right.astype(jnp.bfloat16), preferred_...  62.8 us
    all_gather x2, waiting for transfers between devices, prefix(): lax.all_gather(a.astype(kind), axis)  58.4 us
    unnamed x1, blocking collectives  21.7 us
    all_gather x1, waiting for transfers between devices, shards(): lax.all_gather(diagonal_block_inverse.astype(jnp.bfloat16), 'col', axis=2...  10.5 us
    another operation x1, loops' own time, prefix(): return lax.fori_loop(0, ahead, one, state)  10.3 us
    all_gather x1, waiting for transfers between devices, shards(): lax.all_gather(step_map, 'col', axis=2, tiled=True)  8.76 us
    while x1, local copies, waits for them, and re-layouts, prefix(): return lax.fori_loop(0, ahead, one, state)  6.61 us
  transfers between devices with their start and end apart: 4, of which 3 were waited for; matrix products, arithmetic and copies ran while one was open for 5% of the time, Pallas kernels for 0%

commit v1 on v0

v1 whole, which is shorter than its diff:
```python
import functools
import jax
import jax.numpy as jnp
from jax import lax
from jax.experimental import pallas as pl
from jax.experimental.pallas import tpu as pltpu
from jax.sharding import PartitionSpec as P

MESH = pl.DeviceIdType.MESH
F32 = jnp.float32
BF16 = jnp.bfloat16
G0, G1, DH1, H0, GC, XP, XPF, XG, XGF, M1X, M0X, CH, CHO, YF = range(14)
COPIES = 14


def mm(left, right):
    return jnp.dot(left, right, preferred_element_type=F32)


def mt(left, right):
    return lax.dot_general(left, right, (((0,), (0,)), ((), ())), preferred_element_type=F32)


def kernel(
    d_ref, g_ref, h_ref, a_ref, out_ref, cross_ref,
    g0f, g1f, dh1f, h0f, gk, pk, t0, t1, p1f, g1cf, m1, m0, pm1, pm0, yin, ys, kb,
    send, recv,
):
    rows = g0f.shape[1]
    wide = g0f.shape[2]
    tall = gk.shape[1]
    tm = lax.axis_index("tm")
    c = lax.axis_index("col")
    o = 1 - c
    pairs = lax.axis_size("tm") // 2
    k = tm // 2
    even = tm % 2 == 0
    odd = tm % 2 == 1
    last = k == pairs - 1
    mate = {"col": o}
    across = {"tm": tm + 1 - 2 * (tm % 2)}

    def copy(which, src, dst, device):
        return pltpu.make_async_remote_copy(
            src_ref=src, dst_ref=dst, send_sem=send.at[which], recv_sem=recv.at[which],
            device_id=device, device_id_type=MESH,
        )

    barrier = pltpu.get_barrier_semaphore()

    def greet(device):
        pl.semaphore_signal(barrier, inc=1, device_id=device, device_id_type=MESH)

    greet(mate)
    greet(across)

    @pl.when(even & (k > 0))
    def _():
        greet({"tm": tm - 2})
        greet({"tm": tm - 1})

    @pl.when(even & jnp.logical_not(last))
    def _():
        greet({"tm": tm + 2})

    @pl.when(odd & jnp.logical_not(last))
    def _():
        greet({"tm": tm + 1})

    g0f[c] = g_ref[0]
    g1f[c] = g_ref[1]
    dh1f[c, :rows] = d_ref[1].astype(BF16)
    dh1f[c, rows:] = h_ref[1]
    h0f[c] = h_ref[0]

    before = jnp.where(even & (k > 0), 2, 0)
    after = jnp.where(last, 0, 1)
    pl.semaphore_wait(barrier, 2 + before + after)

    first = [
        copy(DH1, dh1f.at[c], dh1f.at[c], mate),
        copy(G0, g0f.at[c], g0f.at[c], mate),
        copy(G1, g1f.at[c], g1f.at[c], mate),
    ]
    for one in first:
        one.start()
    first[0].wait_recv()

    def times(left, span, right):
        return mm(left[0, span], right[:wide]) + mm(left[1, span], right[wide:])

    body = pl.ds(0, rows)
    foot = pl.ds(rows, tall - rows)
    whole = pl.ds(0, tall)

    own0 = g_ref[0]
    w = times(dh1f, whole, own0)
    wb = w[:rows].astype(BF16)
    kappa = w[rows:] - h_ref[0].astype(F32)
    first[1].wait_recv()
    for j in range(2):
        span = pl.ds(j * wide, wide)
        pm0[span] = d_ref[0, span] + mt(g0f[j], wb)
    pk[:rows] = pm0[...].astype(BF16)
    pk[rows:] = kappa.astype(BF16)

    def out_p():
        return copy(XP, pk, p1f.at[c], across)

    @pl.when(odd)
    def _():
        out_p().start()

    first[2].wait_recv()
    gk[c, :rows] = times(g1f, body, own0).astype(BF16)
    gk[c, rows:] = kappa.astype(BF16)

    def out_g():
        return copy(XG, gk.at[c], g1cf.at[c], across)

    @pl.when(odd)
    def _():
        out_g().start()

    join = copy(GC, gk.at[c], gk.at[c], mate)
    join.start()
    join.wait_recv()
    for j in range(2):
        t0[pl.ds(j * wide, wide), :] = gk[j, :rows].T
        t1[pl.ds(j * wide, wide), :] = g1f[j].T

    def chain_even():
        return copy(CH, ys, yin.at[c], {"tm": tm - 2})

    def chain_odd():
        return copy(CHO, ys, yin.at[c], {"tm": tm - 1})

    def in_y():
        return copy(CH, ys, yin.at[c], across)

    def in_yo():
        return copy(CHO, ys, yin.at[c], across)

    @pl.when(odd)
    def _():
        m0[...] = gk[...]
        m1[:, :rows] = g1f[...]
        m1[:, rows:] = -dh1f[:, rows:]
        pm1[...] = d_ref[1]

    @pl.when(even)
    def _():
        out_p().wait_recv()
        ahead = copy(XPF, p1f.at[c], p1f.at[c], mate)
        ahead.start()
        ahead.wait_recv()
        own = gk[c, :rows]
        w = times(p1f, whole, own)
        wb = w[:rows].astype(BF16)
        kz = (w[rows:] + gk[c, rows:].astype(F32)).astype(BF16)
        m0[c, rows:] = kz
        for j in range(2):
            span = pl.ds(j * wide, wide)
            pm0[span] += mm(t0[span, :], wb)

        @pl.when(last & (k > 0))
        def _():
            ys[:rows] = pm0[...].astype(BF16)
            ys[rows:] = kz
            chain_even().start()
            chain_odd().start()

        w1 = times(p1f, whole, g_ref[1])
        wb1 = w1[:rows].astype(BF16)
        m1[c, rows:] = (-(w1[rows:] + h_ref[1].astype(F32))).astype(BF16)
        for j in range(2):
            span = pl.ds(j * wide, wide)
            pm1[span] = d_ref[1, span] + mm(t1[span, :], wb1)
        out_g().wait_recv()
        ahead_g = copy(XGF, g1cf.at[c], g1cf.at[c], mate)
        ahead_g.start()
        ahead_g.wait_recv()
        m0[c, :rows] = times(g1cf, body, own).astype(BF16)
        m0x = copy(M0X, m0.at[c], m0.at[c], mate)
        m0x.start()
        m1[c, :rows] = times(g1cf, body, g_ref[1]).astype(BF16)
        m1x = copy(M1X, m1.at[c], m1.at[c], mate)
        m1x.start()
        m0x.wait_recv()
        m1x.wait_recv()
        for j in range(2):
            t0[pl.ds(j * wide, wide), :] = m0[j, :rows].T
            t1[pl.ds(j * wide, wide), :] = m1[j, :rows].T
        ahead.wait_send()
        ahead_g.wait_send()
        m0x.wait_send()
        m1x.wait_send()

    @pl.when(odd)
    def _():
        out_p().wait_send()
        out_g().wait_send()

    @pl.when(last)
    def _():
        yin[...] = jnp.zeros_like(yin)

    @pl.when(jnp.logical_not(last))
    def _():
        @pl.when(even)
        def _():
            in_y().wait_recv()

        @pl.when(odd)
        def _():
            in_yo().wait_recv()

        ahead = copy(YF, yin.at[c], yin.at[c], mate)
        ahead.start()
        ahead.wait()

    cov = a_ref[...].astype(BF16)

    def apply(step, sign, m, t, p):
        for j in range(2):
            part = times(yin, foot, m[j, :rows])
            kb[j] = sign * part + m[j, rows:].astype(F32)
        w = times(yin, body, m[c, :rows]).astype(BF16)
        for j in range(2):
            span = pl.ds(j * wide, wide)
            p[span] += mm(t[span, :], w)

    def emit(step, p):
        edge = mm(cov, kb[c].astype(BF16))
        cross_ref[step] = edge
        edge = edge.astype(BF16)
        for j in range(2):
            span = pl.ds(j * wide, wide)
            out_ref[step, span] = p[span] + mt(kb[j].astype(BF16), edge)

    apply(0, 1.0, m0, t0, pm0)

    @pl.when(even & (k > 0) & jnp.logical_not(last))
    def _():
        ys[:rows] = pm0[...].astype(BF16)
        ys[rows:] = kb[c].astype(BF16)
        chain_even().start()
        chain_odd().start()

    emit(0, pm0)
    apply(1, -1.0, m1, t1, pm1)
    emit(1, pm1)
    for one in first:
        one.wait_send()
    join.wait_send()

    @pl.when(even & (k > 0))
    def _():
        chain_even().wait_send()
        chain_odd().wait_send()


def shards(diagonal_block_inverse, step_map, arrow_map, arrow_cov):
    count, nodes, wide = diagonal_block_inverse.shape
    effects = arrow_map.shape[1]
    tall = nodes + effects
    vmem = pl.BlockSpec(memory_space=pltpu.VMEM)
    return pl.pallas_call(
        kernel,
        out_shape=(
            jax.ShapeDtypeStruct((count, nodes, wide), F32),
            jax.ShapeDtypeStruct((count, effects, wide), F32),
        ),
        in_specs=[vmem] * 4,
        out_specs=(vmem, vmem),
        scratch_shapes=[
            pltpu.VMEM((2, nodes, wide), BF16),
            pltpu.VMEM((2, nodes, wide), BF16),
            pltpu.VMEM((2, tall, wide), BF16),
            pltpu.VMEM((2, effects, wide), BF16),
            pltpu.VMEM((2, tall, wide), BF16),
            pltpu.VMEM((tall, wide), BF16),
            pltpu.VMEM((nodes, nodes), BF16),
            pltpu.VMEM((nodes, nodes), BF16),
            pltpu.VMEM((2, tall, wide), BF16),
            pltpu.VMEM((2, tall, wide), BF16),
            pltpu.VMEM((2, tall, wide), BF16),
            pltpu.VMEM((2, tall, wide), BF16),
            pltpu.VMEM((nodes, wide), F32),
            pltpu.VMEM((nodes, wide), F32),
            pltpu.VMEM((2, tall, wide), BF16),
            pltpu.VMEM((tall, wide), BF16),
            pltpu.VMEM((2, effects, wide), F32),
            pltpu.SemaphoreType.DMA((COPIES,)),
            pltpu.SemaphoreType.DMA((COPIES,)),
        ],
        compiler_params=pltpu.CompilerParams(
            collective_id=0, has_side_effects=True, vmem_limit_bytes=48 * 1024 * 1024
        ),
    )(diagonal_block_inverse, step_map, arrow_map, arrow_cov)


def solution(mesh):
    return jax.shard_map(
        shards,
        mesh=mesh,
        in_specs=(
            P(("rep", "tm"), None, "col"),
            P(("rep", "tm"), None, "col"),
            P(("rep", "tm"), None, "col"),
            P("rep", None),
        ),
        out_specs=(P(("rep", "tm"), None, "col"), P(("rep", "tm"), None, "col")),
        check_vma=False,
    )
```

time: 278 us -> 60.1 us (0.22)
  the two profiles are of different devices: /device:TPU:0 before, /device:TPU:3 now
where the time goes in v1:
time: 60.1 us; the launch traced here: 59.8 us
  Pallas kernels  53.8 us (90%)
  local copies, waits for them, and re-layouts  5.33 us (9%)
  between operations  0.65 us (1%)
    pallas_call x1, Pallas kernels, shards(): pl.pallas_call(kernel, out_shape=(jax.ShapeDtypeStruct((count, nodes, wid...  53.8 us
    unnamed x10, local copies, waits for them, and re-layouts  5.33 us

profile of v1, /device:TPU:3, one launch (start us, length us, event | category | flops | bytes accessed | tf_op | source)
XLA Modules:
  0.0 59.8 jit_solution(17328075624877168043)
XLA Ops:
  0.6 0.0 copy-start
  0.6 1.2 %copy-done = f32[2,512,256]{2,1,0:T(8,128)S(1)} copy-done((f32[2,512,256]{2,1,0:T(8,128)S(1)}, f32[2,512,256]{2,1,0:T(8,128)}, u32[]{:S(2)}) %copy-start) | copy-done | bytes 1048600
  1.9 0.0 copy-start.1
  1.9 1.0 %copy-done.1 = bf16[2,512,256]{2,1,0:T(8,128)(2,1)S(1)} copy-done((bf16[2,512,256]{2,1,0:T(8,128)(2,1)S(1)}, bf16[2,512,256]{2,1,0:T(8,128)(2,1)}, u32[]{:S(2)}) %copy-start.1) | copy-done | bytes 524312
  2.9 0.0 copy-start.2
  2.9 0.8 %copy-done.2 = bf16[2,32,256]{2,1,0:T(8,128)(2,1)S(1)} copy-done((bf16[2,32,256]{2,1,0:T(8,128)(2,1)S(1)}, bf16[2,32,256]{2,1,0:T(8,128)(2,1)}, u32[]{:S(2)}) %copy-start.2) | copy-done | bytes 32792
  3.7 0.0 copy-start.3
  3.7 0.7 %copy-done.3 = f32[32,32]{1,0:T(8,128)S(1)} copy-done((f32[32,32]{1,0:T(8,128)S(1)}, f32[32,32]{1,0:T(8,128)}, u32[]{:S(2)}) %copy-start.3) | copy-done | bytes 4120
  4.4 53.8 %shard_map.59 = (f32[2,512,256]{2,1,0:T(8,128)S(1)}, f32[2,32,256]{2,1,0:T(8,128)S(1)}) custom-call(f32[2,512,256]{2,1,0:T(8,128)S(1)} %copy-done, bf16[2,512,256]{2,1,0:T(8,128)(2,1)S(1)} %copy-done.1, bf16[2,32,256]{2,1,0:T(8,128)(2,1)S(1)} %copy-done.2, f32[32,32]{1,0:T(8,128)S(1)} %copy-done.3), custom_call_target="tpu_custom_call" | custom-call | tf_op jit(solution)/shard_map/pallas_call | solution.py:268
  58.1 1.0 %copy.8 = f32[2,512,256]{2,1,0:T(8,128)} copy(f32[2,512,256]{2,1,0:T(8,128)S(1)} %get-tuple-element.4) | data formatting | bytes 2097152
  59.1 0.6 %copy.9 = f32[2,32,256]{2,1,0:T(8,128)} copy(f32[2,32,256]{2,1,0:T(8,128)S(1)} %get-tuple-element.5) | data formatting | bytes 131072
Async XLA Ops:
  0.6 1.2 %copy-start = (f32[2,512,256]{2,1,0:T(8,128)S(1)}, f32[2,512,256]{2,1,0:T(8,128)}, u32[]{:S(2)}) copy-start(f32[2,512,256]{2,1,0:T(8,128)} %d_ref.1) | copy-start | bytes 3145732
  1.9 1.0 %copy-start.1 = (bf16[2,512,256]{2,1,0:T(8,128)(2,1)S(1)}, bf16[2,512,256]{2,1,0:T(8,128)(2,1)}, u32[]{:S(2)}) copy-start(bf16[2,512,256]{2,1,0:T(8,128)(2,1)} %g_ref.1) | copy-start | bytes 1572868
  2.9 0.8 %copy-start.2 = (bf16[2,32,256]{2,1,0:T(8,128)(2,1)S(1)}, bf16[2,32,256]{2,1,0:T(8,128)(2,1)}, u32[]{:S(2)}) copy-start(bf16[2,32,256]{2,1,0:T(8,128)(2,1)} %h_ref.1) | copy-start | bytes 98308
  3.7 0.7 %copy-start.3 = (f32[32,32]{1,0:T(8,128)S(1)}, f32[32,32]{1,0:T(8,128)}, u32[]{:S(2)}) copy-start(f32[32,32]{1,0:T(8,128)} %a_ref.1) | copy-start | bytes 12292

commit v2 on v1

v2 whole, which is shorter than its diff:
```python
import functools
import jax
import jax.numpy as jnp
from jax import lax
from jax.experimental import pallas as pl
from jax.experimental.pallas import tpu as pltpu
from jax.sharding import PartitionSpec as P

MESH = pl.DeviceIdType.MESH
F32 = jnp.float32
BF16 = jnp.bfloat16
G0, G1, DH1, GC, XA, XB, XFA, XFB, XG, XGF, M1X, M0X, YA, YB, OA, OB, FA, FB = range(18)
COPIES = 18


def mm(left, right):
    return jnp.dot(left, right, preferred_element_type=F32)


def mt(left, right):
    return lax.dot_general(left, right, (((0,), (0,)), ((), ())), preferred_element_type=F32)


def kernel(
    d_hbm, g_hbm, h_hbm, a_hbm, out_ref, cross_ref,
    d_ref, h_ref, a_ref, g0f, g1f, dh1f, gk, t0, t1, zs, zp, zy, p1f, g1cf, m1, m0, pm1, pm0,
    yin, kb, send, recv, load,
):
    rows = g0f.shape[1]
    wide = g0f.shape[2]
    tall = gk.shape[1]
    half = wide // 2
    early = 3 * half
    edge_rows = tall - rows
    tm = lax.axis_index("tm")
    c = lax.axis_index("col")
    o = 1 - c
    pairs = lax.axis_size("tm") // 2
    k = tm // 2
    even = tm % 2 == 0
    odd = tm % 2 == 1
    last = k == pairs - 1
    mate = {"col": o}
    across = {"tm": tm + 1 - 2 * (tm % 2)}

    def copy(which, src, dst, device):
        return pltpu.make_async_remote_copy(
            src_ref=src, dst_ref=dst, send_sem=send.at[which], recv_sem=recv.at[which],
            device_id=device, device_id_type=MESH,
        )

    loads = [
        pltpu.make_async_copy(d_hbm.at[1], d_ref.at[1], load.at[0]),
        pltpu.make_async_copy(h_hbm, h_ref, load.at[1]),
        pltpu.make_async_copy(g_hbm.at[0], g0f.at[c], load.at[2]),
        pltpu.make_async_copy(g_hbm.at[1], g1f.at[c], load.at[3]),
        pltpu.make_async_copy(d_hbm.at[0], d_ref.at[0], load.at[4]),
        pltpu.make_async_copy(a_hbm, a_ref, load.at[5]),
    ]
    for one in loads:
        one.start()

    barrier = pltpu.get_barrier_semaphore()

    def greet(device):
        pl.semaphore_signal(barrier, inc=1, device_id=device, device_id_type=MESH)

    greet(mate)
    greet(across)

    @pl.when(even & (k > 0))
    def _():
        greet({"tm": tm - 2})

    @pl.when(even & jnp.logical_not(last))
    def _():
        greet({"tm": tm + 2})

    loads[0].wait()
    loads[1].wait()
    dh1f[c, :rows] = d_ref[1].astype(BF16)
    dh1f[c, rows:] = h_ref[1]

    before = jnp.where(even & (k > 0), 1, 0)
    after = jnp.where(even & jnp.logical_not(last), 1, 0)
    pl.semaphore_wait(barrier, 2 + before + after)

    first = [
        copy(DH1, dh1f.at[c], dh1f.at[c], mate),
        copy(G0, g_hbm.at[0], g0f.at[c], mate),
        copy(G1, g_hbm.at[1], g1f.at[c], mate),
    ]
    for one in first:
        one.start()
    for one in loads[2:]:
        one.wait()
    first[0].wait_recv()

    def times(left, span, right):
        return mm(jnp.concatenate([left[0, span], left[1, span]], axis=1), right)

    body = pl.ds(0, rows)
    whole = pl.ds(0, tall)

    def pack(p, edge):
        r = pl.multiple_of(c * wide, wide)
        zs[:half] = p[pl.ds(r, half), :half].astype(BF16)
        zs[half : 2 * half] = p[pl.ds(r + half, half), half:].astype(BF16)
        zs[2 * half : early] = p[pl.ds(r, half), half:].astype(BF16)

        @pl.when(c == 0)
        def _():
            zs[early : 4 * half] = p[wide : wide + half, :half].astype(BF16)
            zs[4 * half : 5 * half] = p[wide + half :, :half].astype(BF16)

        @pl.when(c == 1)
        def _():
            zs[early : 4 * half] = p[half:wide, :half].astype(BF16)
            zs[4 * half : 5 * half] = p[half:wide, half:].astype(BF16)

        zs[5 * half : 5 * half + edge_rows] = edge[:, :half].astype(BF16)
        zs[5 * half + edge_rows :] = edge[:, half:].astype(BF16)

    def unpack(z, full):
        for j in range(2):
            base = j * wide
            lo = pl.ds(base, half)
            hi = pl.ds(base + half, half)
            full[lo, lo] = z[j, :half]
            full[hi, hi] = z[j, half : 2 * half]
            inner = z[j, 2 * half : early]
            full[lo, hi] = inner
            full[hi, lo] = inner.T
            for n in range(2):
                outer = z[j, early + n * half : early + (n + 1) * half]
                far = pl.ds(wide + n * half, half)
                near = pl.ds(j * half, half)
                if j == 0:
                    full[far, near] = outer
                    full[near, far] = outer.T
                else:
                    full[near, far] = outer
                    full[far, near] = outer.T
                full[rows:, pl.ds(base + n * half, half)] = z[
                    j, 5 * half + n * edge_rows : 5 * half + (n + 1) * edge_rows
                ]

    top = pl.ds(0, early)
    low = pl.ds(early, zs.shape[0] - early)

    def pieces(ids, src, dst, device):
        return [
            copy(ids[0], src.at[top], dst.at[top], device),
            copy(ids[1], src.at[low], dst.at[low], device),
        ]

    own0 = g0f[c]
    w = times(dh1f, whole, own0)
    wb = w[:rows].astype(BF16)
    kappa = w[rows:] - h_ref[0].astype(F32)
    first[1].wait_recv()
    for j in range(2):
        span = pl.ds(j * wide, wide)
        pm0[span] = d_ref[0, span] + mt(g0f[j], wb)

    out_p = pieces((XA, XB), zs, zp.at[c], across)

    @pl.when(odd)
    def _():
        pack(pm0, kappa)
        for one in out_p:
            one.start()

    first[2].wait_recv()
    gk[c, :rows] = times(g1f, body, own0).astype(BF16)
    gk[c, rows:] = kappa.astype(BF16)
    out_g = copy(XG, gk.at[c], g1cf.at[c], across)

    @pl.when(odd)
    def _():
        out_g.start()

    join = copy(GC, gk.at[c], gk.at[c], mate)
    join.start()
    join.wait_recv()
    for j in range(2):
        t0[pl.ds(j * wide, wide), :] = gk[j, :rows].T
        t1[pl.ds(j * wide, wide), :] = g1f[j].T

    chain = pieces((YA, YB), zs, zy.at[c], {"tm": tm - 2})

    @pl.when(odd)
    def _():
        m0[...] = gk[...]
        m1[:, :rows] = g1f[...]
        m1[:, rows:] = -dh1f[:, rows:]
        pm1[...] = d_ref[1]

    @pl.when(even)
    def _():
        ahead = pieces((XFA, XFB), zp.at[c], zp.at[c], mate)
        for one, two in zip(out_p, ahead):
            one.wait_recv()
            two.start()
        for two in ahead:
            two.wait_recv()
        unpack(zp, p1f)
        own = gk[c, :rows]
        w = mm(p1f[...], own)
        wb = w[:rows].astype(BF16)
        kz = w[rows:] + gk[c, rows:].astype(F32)
        m0[c, rows:] = kz.astype(BF16)
        for j in range(2):
            span = pl.ds(j * wide, wide)
            pm0[span] += mm(t0[span, :], wb)

        @pl.when(last & (k > 0))
        def _():
            pack(pm0, kz)
            for one in chain:
                one.start()

        w1 = mm(p1f[...], g1f[c])
        wb1 = w1[:rows].astype(BF16)
        m1[c, rows:] = (-(w1[rows:] + h_ref[1].astype(F32))).astype(BF16)
        for j in range(2):
            span = pl.ds(j * wide, wide)
            pm1[span] = d_ref[1, span] + mm(t1[span, :], wb1)
        out_g.wait_recv()
        ahead_g = copy(XGF, g1cf.at[c], g1cf.at[c], mate)
        ahead_g.start()
        ahead_g.wait_recv()
        m0[c, :rows] = times(g1cf, body, own).astype(BF16)
        m0x = copy(M0X, m0.at[c], m0.at[c], mate)
        m0x.start()
        m1[c, :rows] = times(g1cf, body, g1f[c]).astype(BF16)
        m1x = copy(M1X, m1.at[c], m1.at[c], mate)
        m1x.start()
        m0x.wait_recv()
        m1x.wait_recv()
        for j in range(2):
            t0[pl.ds(j * wide, wide), :] = m0[j, :rows].T
            t1[pl.ds(j * wide, wide), :] = m1[j, :rows].T
        for two in ahead:
            two.wait_send()
        ahead_g.wait_send()
        m0x.wait_send()
        m1x.wait_send()

    @pl.when(odd)
    def _():
        for one in out_p:
            one.wait_send()
        out_g.wait_send()

    beside = pieces((OA, OB), zy.at[c], zy.at[c], across)
    inner = pieces((FA, FB), zy.at[c], zy.at[c], mate)

    @pl.when(last)
    def _():
        yin[...] = jnp.zeros_like(yin)

    @pl.when(jnp.logical_not(last))
    def _():
        @pl.when(even)
        def _():
            for n in range(2):
                chain[n].wait_recv()
                inner[n].start()
                beside[n].start()

        @pl.when(odd)
        def _():
            for n in range(2):
                beside[n].wait_recv()
                inner[n].start()

        for one in inner:
            one.wait_recv()
        unpack(zy, yin)

    cov = a_ref[...].astype(BF16)

    def edges(sign, m):
        for j in range(2):
            kb[j] = sign * mm(yin[rows:], m[j, :rows]) + m[j, rows:].astype(F32)

    def apply(m, t, p):
        w = mm(yin[:rows], m[c, :rows]).astype(BF16)
        for j in range(2):
            span = pl.ds(j * wide, wide)
            p[span] += mm(t[span, :], w)

    def emit(step, p):
        edge = mm(cov, kb[c].astype(BF16))
        cross_ref[step] = edge
        edge = edge.astype(BF16)
        for j in range(2):
            span = pl.ds(j * wide, wide)
            out_ref[step, span] = p[span] + mt(kb[j].astype(BF16), edge)

    edges(1.0, m0)
    apply(m0, t0, pm0)

    @pl.when(even & (k > 0) & jnp.logical_not(last))
    def _():
        pack(pm0, kb[c])
        for one in chain:
            one.start()

    emit(0, pm0)
    edges(-1.0, m1)
    apply(m1, t1, pm1)
    emit(1, pm1)
    for one in first:
        one.wait_send()
    join.wait_send()

    @pl.when(jnp.logical_not(last))
    def _():
        for one in inner:
            one.wait_send()

    @pl.when(even & jnp.logical_not(last))
    def _():
        for one in beside:
            one.wait_send()

    @pl.when(even & (k > 0))
    def _():
        for one in chain:
            one.wait_send()


def shards(diagonal_block_inverse, step_map, arrow_map, arrow_cov):
    count, nodes, wide = diagonal_block_inverse.shape
    effects = arrow_map.shape[1]
    tall = nodes + effects
    packed = 5 * (wide // 2) + 2 * effects
    vmem = pl.BlockSpec(memory_space=pltpu.VMEM)
    return pl.pallas_call(
        kernel,
        out_shape=(
            jax.ShapeDtypeStruct((count, nodes, wide), F32),
            jax.ShapeDtypeStruct((count, effects, wide), F32),
        ),
        in_specs=[pl.BlockSpec(memory_space=pl.ANY)] * 4,
        out_specs=(vmem, vmem),
        scratch_shapes=[
            pltpu.VMEM((count, nodes, wide), F32),
            pltpu.VMEM((count, effects, wide), BF16),
            pltpu.VMEM((effects, effects), F32),
            pltpu.VMEM((2, nodes, wide), BF16),
            pltpu.VMEM((2, nodes, wide), BF16),
            pltpu.VMEM((2, tall, wide), BF16),
            pltpu.VMEM((2, tall, wide), BF16),
            pltpu.VMEM((nodes, nodes), BF16),
            pltpu.VMEM((nodes, nodes), BF16),
            pltpu.VMEM((packed, wide // 2), BF16),
            pltpu.VMEM((2, packed, wide // 2), BF16),
            pltpu.VMEM((2, packed, wide // 2), BF16),
            pltpu.VMEM((tall, nodes), BF16),
            pltpu.VMEM((2, tall, wide), BF16),
            pltpu.VMEM((2, tall, wide), BF16),
            pltpu.VMEM((2, tall, wide), BF16),
            pltpu.VMEM((nodes, wide), F32),
            pltpu.VMEM((nodes, wide), F32),
            pltpu.VMEM((tall, nodes), BF16),
            pltpu.VMEM((2, effects, wide), F32),
            pltpu.SemaphoreType.DMA((COPIES,)),
            pltpu.SemaphoreType.DMA((COPIES,)),
            pltpu.SemaphoreType.DMA((6,)),
        ],
        compiler_params=pltpu.CompilerParams(
            collective_id=0, has_side_effects=True, vmem_limit_bytes=48 * 1024 * 1024
        ),
    )(diagonal_block_inverse, step_map, arrow_map, arrow_cov)


def solution(mesh):
    return jax.shard_map(
        shards,
        mesh=mesh,
        in_specs=(
            P(("rep", "tm"), None, "col"),
            P(("rep", "tm"), None, "col"),
            P(("rep", "tm"), None, "col"),
            P("rep", None),
        ),
        out_specs=(P(("rep", "tm"), None, "col"), P(("rep", "tm"), None, "col")),
        check_vma=False,
    )
```

time: 60.1 us -> 50 us (0.83)
  Pallas kernels: 53.8 us -> 43.7 us
    pallas_call x1, Pallas kernels: 53.8 us -> 43.7 us  [shards(): pl.pallas_call(kernel, out_shape=(jax.ShapeDtypeStruct((count, nodes, wid...]
where the time goes in v2:
time: 50 us; the launch traced here: 49.7 us
  Pallas kernels  43.7 us (87%)
  local copies, waits for them, and re-layouts  5.33 us (11%)
  between operations  0.65 us (1%)
    pallas_call x1, Pallas kernels, shards(): pl.pallas_call(kernel, out_shape=(jax.ShapeDtypeStruct((count, nodes, wid...  43.7 us
    unnamed x10, local copies, waits for them, and re-layouts  5.33 us

profile of v2, /device:TPU:3, one launch (start us, length us, event | category | flops | bytes accessed | tf_op | source)
XLA Modules:
  0.0 49.7 jit_solution(2741788244272070712)
XLA Ops:
  0.6 0.0 copy-start
  0.6 1.2 %copy-done = f32[2,512,256]{2,1,0:T(8,128)S(1)} copy-done((f32[2,512,256]{2,1,0:T(8,128)S(1)}, f32[2,512,256]{2,1,0:T(8,128)}, u32[]{:S(2)}) %copy-start) | copy-done | bytes 1048600
  1.9 0.0 copy-start.1
  1.9 1.0 %copy-done.1 = bf16[2,512,256]{2,1,0:T(8,128)(2,1)S(1)} copy-done((bf16[2,512,256]{2,1,0:T(8,128)(2,1)S(1)}, bf16[2,512,256]{2,1,0:T(8,128)(2,1)}, u32[]{:S(2)}) %copy-start.1) | copy-done | bytes 524312
  2.9 0.0 copy-start.2
  2.9 0.8 %copy-done.2 = bf16[2,32,256]{2,1,0:T(8,128)(2,1)S(1)} copy-done((bf16[2,32,256]{2,1,0:T(8,128)(2,1)S(1)}, bf16[2,32,256]{2,1,0:T(8,128)(2,1)}, u32[]{:S(2)}) %copy-start.2) | copy-done | bytes 32792
  3.7 0.0 copy-start.3
  3.7 0.7 %copy-done.3 = f32[32,32]{1,0:T(8,128)S(1)} copy-done((f32[32,32]{1,0:T(8,128)S(1)}, f32[32,32]{1,0:T(8,128)}, u32[]{:S(2)}) %copy-start.3) | copy-done | bytes 4120
  4.4 43.7 %shard_map.59 = (f32[2,512,256]{2,1,0:T(8,128)S(1)}, f32[2,32,256]{2,1,0:T(8,128)S(1)}) custom-call(f32[2,512,256]{2,1,0:T(8,128)S(1)} %copy-done, bf16[2,512,256]{2,1,0:T(8,128)(2,1)S(1)} %copy-done.1, bf16[2,32,256]{2,1,0:T(8,128)(2,1)S(1)} %copy-done.2, f32[32,32]{1,0:T(8,128)S(1)} %copy-done.3), custom_call_target="tpu_custom_call" | custom-call | tf_op jit(solution)/shard_map/pallas_call | solution.py:341
  48.1 1.0 %copy.8 = f32[2,512,256]{2,1,0:T(8,128)} copy(f32[2,512,256]{2,1,0:T(8,128)S(1)} %get-tuple-element.4) | data formatting | bytes 2097152
  49.0 0.6 %copy.9 = f32[2,32,256]{2,1,0:T(8,128)} copy(f32[2,32,256]{2,1,0:T(8,128)S(1)} %get-tuple-element.5) | data formatting | bytes 131072
Async XLA Ops:
  0.6 1.2 %copy-start = (f32[2,512,256]{2,1,0:T(8,128)S(1)}, f32[2,512,256]{2,1,0:T(8,128)}, u32[]{:S(2)}) copy-start(f32[2,512,256]{2,1,0:T(8,128)} %d_hbm.1) | copy-start | bytes 3145732
  1.9 1.0 %copy-start.1 = (bf16[2,512,256]{2,1,0:T(8,128)(2,1)S(1)}, bf16[2,512,256]{2,1,0:T(8,128)(2,1)}, u32[]{:S(2)}) copy-start(bf16[2,512,256]{2,1,0:T(8,128)(2,1)} %g_hbm.1) | copy-start | bytes 1572868
  2.9 0.8 %copy-start.2 = (bf16[2,32,256]{2,1,0:T(8,128)(2,1)S(1)}, bf16[2,32,256]{2,1,0:T(8,128)(2,1)}, u32[]{:S(2)}) copy-start(bf16[2,32,256]{2,1,0:T(8,128)(2,1)} %h_hbm.1) | copy-start | bytes 98308
  3.7 0.7 %copy-start.3 = (f32[32,32]{1,0:T(8,128)S(1)}, f32[32,32]{1,0:T(8,128)}, u32[]{:S(2)}) copy-start(f32[32,32]{1,0:T(8,128)} %a_hbm.1) | copy-start | bytes 12292

commit v3 on v2

--- a/solution.py
+++ b/solution.py
@@ -102,26 +102,30 @@
     body = pl.ds(0, rows)
     whole = pl.ds(0, tall)
 
-    def pack(p, edge):
+    mine = pl.ds(pl.multiple_of(c * wide, wide), wide)
+    other = pl.ds(pl.multiple_of(o * wide, wide), wide)
+    first_rows = early + 2 * edge_rows
+
+    def pack_first(p, edge):
         r = pl.multiple_of(c * wide, wide)
         zs[:half] = p[pl.ds(r, half), :half].astype(BF16)
         zs[half : 2 * half] = p[pl.ds(r + half, half), half:].astype(BF16)
         zs[2 * half : early] = p[pl.ds(r, half), half:].astype(BF16)
-
+        zs[early : early + edge_rows] = edge[:, :half].astype(BF16)
+        zs[early + edge_rows : first_rows] = edge[:, half:].astype(BF16)
+
+    def pack_second(p):
         @pl.when(c == 0)
         def _():
-            zs[early : 4 * half] = p[wide : wide + half, :half].astype(BF16)
-            zs[4 * half : 5 * half] = p[wide + half :, :half].astype(BF16)
+            zs[first_rows : first_rows + half] = p[wide : wide + half, :half].astype(BF16)
+            zs[first_rows + half :] = p[wide + half :, :half].astype(BF16)
 
         @pl.when(c == 1)
         def _():
-            zs[early : 4 * half] = p[half:wide, :half].astype(BF16)
-            zs[4 * half : 5 * half] = p[half:wide, half:].astype(BF16)
-
-        zs[5 * half : 5 * half + edge_rows] = edge[:, :half].astype(BF16)
-        zs[5 * half + edge_rows :] = edge[:, half:].astype(BF16)
-
-    def unpack(z, full):
+            zs[first_rows : first_rows + half] = p[half:wide, :half].astype(BF16)
+            zs[first_rows + half :] = p[half:wide, half:].astype(BF16)
+
+    def unpack_first(z, full):
         for j in range(2):
             base = j * wide
             lo = pl.ds(base, half)
@@ -132,21 +136,25 @@
             full[lo, hi] = inner
             full[hi, lo] = inner.T
             for n in range(2):
-                outer = z[j, early + n * half : early + (n + 1) * half]
+                full[rows:, pl.ds(base + n * half, half)] = z[
+                    j, early + n * edge_rows : early + (n + 1) * edge_rows
+                ]
+
+    def unpack_second(z, full):
+        for j in range(2):
+            near = pl.ds(j * half, half)
+            for n in range(2):
+                outer = z[j, first_rows + n * half : first_rows + (n + 1) * half]
                 far = pl.ds(wide + n * half, half)
-                near = pl.ds(j * half, half)
                 if j == 0:
                     full[far, near] = outer
                     full[near, far] = outer.T
                 else:
                     full[near, far] = outer
                     full[far, near] = outer.T
-                full[rows:, pl.ds(base + n * half, half)] = z[
-                    j, 5 * half + n * edge_rows : 5 * half + (n + 1) * edge_rows
-                ]
-
-    top = pl.ds(0, early)
-    low = pl.ds(early, zs.shape[0] - early)
+
+    top = pl.ds(0, first_rows)
+    low = pl.ds(first_rows, zs.shape[0] - first_rows)
 
     def pieces(ids, src, dst, device):
         return [
@@ -158,18 +166,21 @@
     w = times(dh1f, whole, own0)
     wb = w[:rows].astype(BF16)
     kappa = w[rows:] - h_ref[0].astype(F32)
+    pm0[mine] = d_ref[0, mine] + mt(g0f[c], wb)
+    out_p = pieces((XA, XB), zs, zp.at[c], across)
+
+    @pl.when(odd)
+    def _():
+        pack_first(pm0, kappa)
+        out_p[0].start()
+
     first[1].wait_recv()
-    for j in range(2):
-        span = pl.ds(j * wide, wide)
-        pm0[span] = d_ref[0, span] + mt(g0f[j], wb)
-
-    out_p = pieces((XA, XB), zs, zp.at[c], across)
+    pm0[other] = d_ref[0, other] + mt(g0f[o], wb)
 
     @pl.when(odd)
     def _():
-        pack(pm0, kappa)
-        for one in out_p:
-            one.start()
+        pack_second(pm0)
+        out_p[1].start()
 
     first[2].wait_recv()
     gk[c, :rows] = times(g1f, body, own0).astype(BF16)
@@ -202,23 +213,28 @@
         for one, two in zip(out_p, ahead):
             one.wait_recv()
             two.start()
-        for two in ahead:
-            two.wait_recv()
-        unpack(zp, p1f)
+        ahead[0].wait_recv()
+        unpack_first(zp, p1f)
+        ahead[1].wait_recv()
+        unpack_second(zp, p1f)
         own = gk[c, :rows]
         w = mm(p1f[...], own)
         wb = w[:rows].astype(BF16)
         kz = w[rows:] + gk[c, rows:].astype(F32)
         m0[c, rows:] = kz.astype(BF16)
-        for j in range(2):
-            span = pl.ds(j * wide, wide)
-            pm0[span] += mm(t0[span, :], wb)
+        pm0[mine] += mm(t0[mine, :], wb)
 
         @pl.when(last & (k > 0))
         def _():
-            pack(pm0, kz)
-            for one in chain:
-                one.start()
+            pack_first(pm0, kz)
+            chain[0].start()
+
+        pm0[other] += mm(t0[other, :], wb)
+
+        @pl.when(last & (k > 0))
+        def _():
+            pack_second(pm0)
+            chain[1].start()
 
         w1 = mm(p1f[...], g1f[c])
         wb1 = w1[:rows].astype(BF16)
@@ -256,61 +272,76 @@
     beside = pieces((OA, OB), zy.at[c], zy.at[c], across)
     inner = pieces((FA, FB), zy.at[c], zy.at[c], mate)
 
+    cov = a_ref[...].astype(BF16)
+
+    def edges(step, sign, m):
+        for j in range(2):
+            kb[step, j] = sign * mm(yin[rows:], m[j, :rows]) + m[j, rows:].astype(F32)
+
     @pl.when(last)
     def _():
         yin[...] = jnp.zeros_like(yin)
 
+    def relay(n):
+        @pl.when(even)
+        def _():
+            chain[n].wait_recv()
+            inner[n].start()
+            beside[n].start()
+
+        @pl.when(odd)
+        def _():
+            beside[n].wait_recv()
+            inner[n].start()
+
     @pl.when(jnp.logical_not(last))
     def _():
-        @pl.when(even)
-        def _():
-            for n in range(2):
-                chain[n].wait_recv()
-                inner[n].start()
-                beside[n].start()
-
-        @pl.when(odd)
-        def _():
-            for n in range(2):
-                beside[n].wait_recv()
-                inner[n].start()
-
-        for one in inner:
-            one.wait_recv()
-        unpack(zy, yin)
-
-    cov = a_ref[...].astype(BF16)
-
-    def edges(sign, m):
-        for j in range(2):
-            kb[j] = sign * mm(yin[rows:], m[j, :rows]) + m[j, rows:].astype(F32)
-
-    def apply(m, t, p):
-        w = mm(yin[:rows], m[c, :rows]).astype(BF16)
+        relay(0)
+        inner[0].wait_recv()
+        unpack_first(zy, yin)
+
+    edges(0, 1.0, m0)
+    edges(1, -1.0, m1)
+    for step in range(2):
+        kb_edge = mm(cov, kb[step, c].astype(BF16))
+        cross_ref[step] = kb_edge
+
+    @pl.when(jnp.logical_not(last))
+    def _():
+        relay(1)
+        inner[1].wait_recv()
+        unpack_second(zy, yin)
+
+    def state(m):
+        return mm(yin[:rows], m[c, :rows]).astype(BF16)
+
+    def emit(step, p):
+        edge = cross_ref[step].astype(BF16)
         for j in range(2):
             span = pl.ds(j * wide, wide)
-            p[span] += mm(t[span, :], w)
-
-    def emit(step, p):
-        edge = mm(cov, kb[c].astype(BF16))
-        cross_ref[step] = edge
-        edge = edge.astype(BF16)
-        for j in range(2):
-            span = pl.ds(j * wide, wide)
-            out_ref[step, span] = p[span] + mt(kb[j].astype(BF16), edge)
-
-    edges(1.0, m0)
-    apply(m0, t0, pm0)
-
-    @pl.when(even & (k > 0) & jnp.logical_not(last))
-    def _():
-        pack(pm0, kb[c])
-        for one in chain:
-            one.start()
+            out_ref[step, span] = p[span] + mt(kb[step, j].astype(BF16), edge)
+
+    passes = even & (k > 0) & jnp.logical_not(last)
+    w = state(m0)
+    pm0[mine] += mm(t0[mine, :], w)
+
+    @pl.when(passes)
+    def _():
+        pack_first(pm0, kb[0, c])
+        chain[0].start()
+
+    pm0[other] += mm(t0[other, :], w)
+
+    @pl.when(passes)
+    def _():
+        pack_second(pm0)
+        chain[1].start()
 
     emit(0, pm0)
-    edges(-1.0, m1)
-    apply(m1, t1, pm1)
+    w = state(m1)
+    for j in range(2):
+        span = pl.ds(j * wide, wide)
+        pm1[span] += mm(t1[span, :], w)
     emit(1, pm1)
     for one in first:
         one.wait_send()
@@ -344,7 +375,7 @@
             jax.ShapeDtypeStruct((count, nodes, wide), F32),
             jax.ShapeDtypeStruct((count, effects, wide), F32),
         ),
-        in_specs=[pl.BlockSpec(memory_space=pl.ANY)] * 4,
+        in_specs=[pl.BlockSpec(memory_space=pltpu.HBM)] * 4,
         out_specs=(vmem, vmem),
         scratch_shapes=[
             pltpu.VMEM((count, nodes, wide), F32),
@@ -366,7 +397,7 @@
             pltpu.VMEM((nodes, wide), F32),
             pltpu.VMEM((nodes, wide), F32),
             pltpu.VMEM((tall, nodes), BF16),
-            pltpu.VMEM((2, effects, wide), F32),
+            pltpu.VMEM((count, 2, effects, wide), F32),
             pltpu.SemaphoreType.DMA((COPIES,)),
             pltpu.SemaphoreType.DMA((COPIES,)),
             pltpu.SemaphoreType.DMA((6,)),

time: 50 us -> 50.7 us (1.014)
  Pallas kernels: 43.7 us -> 44.4 us
    pallas_call x1, Pallas kernels: 43.7 us -> 44.4 us  [shards(): pl.pallas_call(kernel, out_shape=(jax.ShapeDtypeStruct((count, nodes, wid...]
where the time goes in v3:
time: 50.7 us; the launch traced here: 50.4 us
  Pallas kernels  44.4 us (88%)
  local copies, waits for them, and re-layouts  5.33 us (11%)
  between operations  0.65 us (1%)
    pallas_call x1, Pallas kernels, shards(): pl.pallas_call(kernel, out_shape=(jax.ShapeDtypeStruct((count, nodes, wid...  44.4 us
    unnamed x10, local copies, waits for them, and re-layouts  5.33 us

profile of v3, /device:TPU:3, one launch (start us, length us, event | category | flops | bytes accessed | tf_op | source)
XLA Modules:
  0.0 50.4 jit_solution(2221337565939413576)
XLA Ops:
  0.6 0.0 copy-start
  0.6 1.2 %copy-done = f32[2,512,256]{2,1,0:T(8,128)S(1)} copy-done((f32[2,512,256]{2,1,0:T(8,128)S(1)}, f32[2,512,256]{2,1,0:T(8,128)}, u32[]{:S(2)}) %copy-start) | copy-done | bytes 1048600
  1.9 0.0 copy-start.1
  1.9 1.0 %copy-done.1 = bf16[2,512,256]{2,1,0:T(8,128)(2,1)S(1)} copy-done((bf16[2,512,256]{2,1,0:T(8,128)(2,1)S(1)}, bf16[2,512,256]{2,1,0:T(8,128)(2,1)}, u32[]{:S(2)}) %copy-start.1) | copy-done | bytes 524312
  2.9 0.0 copy-start.2
  2.9 0.8 %copy-done.2 = bf16[2,32,256]{2,1,0:T(8,128)(2,1)S(1)} copy-done((bf16[2,32,256]{2,1,0:T(8,128)(2,1)S(1)}, bf16[2,32,256]{2,1,0:T(8,128)(2,1)}, u32[]{:S(2)}) %copy-start.2) | copy-done | bytes 32792
  3.7 0.0 copy-start.3
  3.7 0.7 %copy-done.3 = f32[32,32]{1,0:T(8,128)S(1)} copy-done((f32[32,32]{1,0:T(8,128)S(1)}, f32[32,32]{1,0:T(8,128)}, u32[]{:S(2)}) %copy-start.3) | copy-done | bytes 4120
  4.4 44.4 %shard_map.59 = (f32[2,512,256]{2,1,0:T(8,128)S(1)}, f32[2,32,256]{2,1,0:T(8,128)S(1)}) custom-call(f32[2,512,256]{2,1,0:T(8,128)S(1)} %copy-done, bf16[2,512,256]{2,1,0:T(8,128)(2,1)S(1)} %copy-done.1, bf16[2,32,256]{2,1,0:T(8,128)(2,1)S(1)} %copy-done.2, f32[32,32]{1,0:T(8,128)S(1)} %copy-done.3), custom_call_target="tpu_custom_call" | custom-call | tf_op jit(solution)/shard_map/pallas_call | solution.py:372
  48.7 1.0 %copy.8 = f32[2,512,256]{2,1,0:T(8,128)} copy(f32[2,512,256]{2,1,0:T(8,128)S(1)} %get-tuple-element.4) | data formatting | bytes 2097152
  49.7 0.6 %copy.9 = f32[2,32,256]{2,1,0:T(8,128)} copy(f32[2,32,256]{2,1,0:T(8,128)S(1)} %get-tuple-element.5) | data formatting | bytes 131072
Async XLA Ops:
  0.6 1.2 %copy-start = (f32[2,512,256]{2,1,0:T(8,128)S(1)}, f32[2,512,256]{2,1,0:T(8,128)}, u32[]{:S(2)}) copy-start(f32[2,512,256]{2,1,0:T(8,128)} %d_hbm.1) | copy-start | bytes 3145732
  1.9 1.0 %copy-start.1 = (bf16[2,512,256]{2,1,0:T(8,128)(2,1)S(1)}, bf16[2,512,256]{2,1,0:T(8,128)(2,1)}, u32[]{:S(2)}) copy-start(bf16[2,512,256]{2,1,0:T(8,128)(2,1)} %g_hbm.1) | copy-start | bytes 1572868
  2.9 0.8 %copy-start.2 = (bf16[2,32,256]{2,1,0:T(8,128)(2,1)S(1)}, bf16[2,32,256]{2,1,0:T(8,128)(2,1)}, u32[]{:S(2)}) copy-start(bf16[2,32,256]{2,1,0:T(8,128)(2,1)} %h_hbm.1) | copy-start | bytes 98308
  3.7 0.7 %copy-start.3 = (f32[32,32]{1,0:T(8,128)S(1)}, f32[32,32]{1,0:T(8,128)}, u32[]{:S(2)}) copy-start(f32[32,32]{1,0:T(8,128)} %a_hbm.1) | copy-start | bytes 12292

commit v4 on v3

--- a/solution.py
+++ b/solution.py
@@ -403,7 +403,7 @@
             pltpu.SemaphoreType.DMA((6,)),
         ],
         compiler_params=pltpu.CompilerParams(
-            collective_id=0, has_side_effects=True, vmem_limit_bytes=48 * 1024 * 1024
+            collective_id=0, has_side_effects=True, vmem_limit_bytes=63 * 1024 * 1024
         ),
     )(diagonal_block_inverse, step_map, arrow_map, arrow_cov)
 

time: 50.7 us -> 49.9 us (0.984)
  local copies, waits for them, and re-layouts: 5.33 us -> 2.93 us
  Pallas kernels: 44.4 us -> 46.2 us
    unnamed x10 -> x4, local copies, waits for them, and re-layouts: 5.33 us -> 2.93 us
    pallas_call x1, Pallas kernels: 44.4 us -> 46.2 us  [shards(): pl.pallas_call(kernel, out_shape=(jax.ShapeDtypeStruct((count, nodes, wid...]
where the time goes in v4:
time: 49.9 us; the launch traced here: 49.8 us
  Pallas kernels  46.2 us (93%)
  local copies, waits for them, and re-layouts  2.93 us (6%)
  between operations  0.65 us (1%)
    pallas_call x1, Pallas kernels, shards(): pl.pallas_call(kernel, out_shape=(jax.ShapeDtypeStruct((count, nodes, wid...  46.2 us
    unnamed x4, local copies, waits for them, and re-layouts  2.93 us

profile of v4, /device:TPU:3, one launch (start us, length us, event | category | flops | bytes accessed | tf_op | source)
XLA Modules:
  0.0 49.8 jit_solution(368910075616711921)
XLA Ops:
  0.6 46.2 %shard_map.59 = (f32[2,512,256]{2,1,0:T(8,128)}, f32[2,32,256]{2,1,0:T(8,128)}) custom-call(f32[2,512,256]{2,1,0:T(8,128)} %d_hbm.1, bf16[2,512,256]{2,1,0:T(8,128)(2,1)} %g_hbm.1, bf16[2,32,256]{2,1,0:T(8,128)(2,1)} %h_hbm.1, f32[32,32]{1,0:T(8,128)} %a_hbm.1), custom_call_target="tpu_custom_call" | custom-call | tf_op jit(solution)/shard_map/pallas_call | solution.py:372
  46.8 0.0 copy-start
  46.8 2.3 %copy.8 = f32[2,512,256]{2,1,0:T(8,128)} copy(f32[2,512,256]{2,1,0:T(8,128)} %get-tuple-element.4) | data formatting | bytes 2097152
  49.1 0.0 copy-done
  49.1 0.6 %copy.9 = f32[2,32,256]{2,1,0:T(8,128)} copy(f32[2,32,256]{2,1,0:T(8,128)S(1)} %copy-done) | data formatting | bytes 131072
Async XLA Ops:
  46.8 2.3 %copy-start = (f32[2,32,256]{2,1,0:T(8,128)S(1)}, f32[2,32,256]{2,1,0:T(8,128)}, u32[]{:S(2)}) copy-start(f32[2,32,256]{2,1,0:T(8,128)} %get-tuple-element.5) | copy-start | bytes 196612

commit v5 on v4

--- a/solution.py
+++ b/solution.py
@@ -9,8 +9,8 @@
 MESH = pl.DeviceIdType.MESH
 F32 = jnp.float32
 BF16 = jnp.bfloat16
-G0, G1, DH1, GC, XA, XB, XFA, XFB, XG, XGF, M1X, M0X, YA, YB, OA, OB, FA, FB = range(18)
-COPIES = 18
+G0, G1, DH1, GC, XA, XB, XFA, XFB, XG, XGF, M1X, M0X, YA, YB, OA, OB, FA, FB, QA, QB, QG, QFA, QFB, QFG, QOA, QOB, QOG, N0, N1, LA, LB = range(31)
+COPIES = 31
 
 
 def mm(left, right):
@@ -24,6 +24,7 @@
 def kernel(
     d_hbm, g_hbm, h_hbm, a_hbm, out_ref, cross_ref,
     d_ref, h_ref, a_ref, g0f, g1f, dh1f, gk, t0, t1, zs, zp, zy, p1f, g1cf, m1, m0, pm1, pm0,
+    zq, zt, gq, pq, n1, n0,
     yin, kb, send, recv, load,
 ):
     rows = g0f.shape[1]
@@ -39,7 +40,11 @@
     k = tm // 2
     even = tm % 2 == 0
     odd = tm % 2 == 1
-    last = k == pairs - 1
+    lower = k % 2 == 0
+    upper = k % 2 == 1
+    last = k >= pairs - 2
+    heads = even & lower & (k > 0)
+    takes = even & upper & jnp.logical_not(last)
     mate = {"col": o}
     across = {"tm": tm + 1 - 2 * (tm % 2)}
 
@@ -68,22 +73,25 @@
     greet(mate)
     greet(across)
 
-    @pl.when(even & (k > 0))
+    @pl.when(heads)
     def _():
         greet({"tm": tm - 2})
 
-    @pl.when(even & jnp.logical_not(last))
+    @pl.when(takes)
     def _():
         greet({"tm": tm + 2})
+
+    @pl.when(even)
+    def _():
+        greet({"tm": tm + 2 - 4 * (k % 2)})
 
     loads[0].wait()
     loads[1].wait()
     dh1f[c, :rows] = d_ref[1].astype(BF16)
     dh1f[c, rows:] = h_ref[1]
 
-    before = jnp.where(even & (k > 0), 1, 0)
-    after = jnp.where(even & jnp.logical_not(last), 1, 0)
-    pl.semaphore_wait(barrier, 2 + before + after)
+    linked = jnp.where(even, 1, 0) + jnp.where(heads | takes, 1, 0)
+    pl.semaphore_wait(barrier, 2 + linked)
 
     first = [
         copy(DH1, dh1f.at[c], dh1f.at[c], mate),
@@ -106,7 +114,7 @@
     other = pl.ds(pl.multiple_of(o * wide, wide), wide)
     first_rows = early + 2 * edge_rows
 
-    def pack_first(p, edge):
+    def pack_first(zs, p, edge):
         r = pl.multiple_of(c * wide, wide)
         zs[:half] = p[pl.ds(r, half), :half].astype(BF16)
         zs[half : 2 * half] = p[pl.ds(r + half, half), half:].astype(BF16)
@@ -114,7 +122,7 @@
         zs[early : early + edge_rows] = edge[:, :half].astype(BF16)
         zs[early + edge_rows : first_rows] = edge[:, half:].astype(BF16)
 
-    def pack_second(p):
+    def pack_second(zs, p):
         @pl.when(c == 0)
         def _():
             zs[first_rows : first_rows + half] = p[wide : wide + half, :half].astype(BF16)
@@ -171,7 +179,7 @@
 
     @pl.when(odd)
     def _():
-        pack_first(pm0, kappa)
+        pack_first(zs, pm0, kappa)
         out_p[0].start()
 
     first[1].wait_recv()
@@ -179,7 +187,7 @@
 
     @pl.when(odd)
     def _():
-        pack_second(pm0)
+        pack_second(zs, pm0)
         out_p[1].start()
 
     first[2].wait_recv()
@@ -199,6 +207,8 @@
         t1[pl.ds(j * wide, wide), :] = g1f[j].T
 
     chain = pieces((YA, YB), zs, zy.at[c], {"tm": tm - 2})
+    pair_up = pieces((QA, QB), zt, zq.at[c], {"tm": tm - 2})
+    pair_map = copy(QG, m0.at[c, body], gq.at[c], {"tm": tm - 2})
 
     @pl.when(odd)
     def _():
@@ -224,17 +234,17 @@
         m0[c, rows:] = kz.astype(BF16)
         pm0[mine] += mm(t0[mine, :], wb)
 
-        @pl.when(last & (k > 0))
-        def _():
-            pack_first(pm0, kz)
-            chain[0].start()
+        @pl.when(upper)
+        def _():
+            pack_first(zt, pm0, kz)
+            pair_up[0].start()
 
         pm0[other] += mm(t0[other, :], wb)
 
-        @pl.when(last & (k > 0))
-        def _():
-            pack_second(pm0)
-            chain[1].start()
+        @pl.when(upper)
+        def _():
+            pack_second(zt, pm0)
+            pair_up[1].start()
 
         w1 = mm(p1f[...], g1f[c])
         wb1 = w1[:rows].astype(BF16)
@@ -249,6 +259,11 @@
         m0[c, :rows] = times(g1cf, body, own).astype(BF16)
         m0x = copy(M0X, m0.at[c], m0.at[c], mate)
         m0x.start()
+
+        @pl.when(upper)
+        def _():
+            pair_map.start()
+
         m1[c, :rows] = times(g1cf, body, g1f[c]).astype(BF16)
         m1x = copy(M1X, m1.at[c], m1.at[c], mate)
         m1x.start()
@@ -269,6 +284,99 @@
             one.wait_send()
         out_g.wait_send()
 
+    @pl.when(upper)
+    def _():
+        n0[...] = m0[...]
+        n1[...] = m1[...]
+
+    side_q = pieces((QOA, QOB), zq.at[c], zq.at[c], across)
+    mate_q = pieces((QFA, QFB), zq.at[c], zq.at[c], mate)
+    side_g = copy(QOG, gq.at[c], gq.at[c], across)
+    mate_g = copy(QFG, gq.at[c], gq.at[c], mate)
+    grown = [copy(N0, n0.at[c], n0.at[c], mate), copy(N1, n1.at[c], n1.at[c], mate)]
+
+    @pl.when(lower)
+    def _():
+        for n in range(2):
+
+            @pl.when(even)
+            def _():
+                pair_up[n].wait_recv()
+                mate_q[n].start()
+                side_q[n].start()
+
+            @pl.when(odd)
+            def _():
+                side_q[n].wait_recv()
+                mate_q[n].start()
+
+        mate_q[0].wait_recv()
+        unpack_first(zq, pq)
+        mate_q[1].wait_recv()
+        unpack_second(zq, pq)
+        w = mm(pq[...], m0[c, :rows])
+        wb = w[:rows].astype(BF16)
+        kq = w[rows:] + m0[c, rows:].astype(F32)
+        n0[c, rows:] = kq.astype(BF16)
+        pm0[mine] += mm(t0[mine, :], wb)
+
+        @pl.when(heads & last)
+        def _():
+            pack_first(zs, pm0, kq)
+            chain[0].start()
+
+        pm0[other] += mm(t0[other, :], wb)
+
+        @pl.when(heads & last)
+        def _():
+            pack_second(zs, pm0)
+            chain[1].start()
+
+        w = mm(pq[...], m1[c, :rows])
+        wb = w[:rows].astype(BF16)
+        n1[c, rows:] = (m1[c, rows:].astype(F32) - w[rows:]).astype(BF16)
+        for j in range(2):
+            span = pl.ds(j * wide, wide)
+            pm1[span] += mm(t1[span, :], wb)
+
+        @pl.when(even)
+        def _():
+            pair_map.wait_recv()
+            mate_g.start()
+            side_g.start()
+
+        @pl.when(odd)
+        def _():
+            side_g.wait_recv()
+            mate_g.start()
+
+        mate_g.wait_recv()
+        n0[c, :rows] = times(gq, body, m0[c, :rows]).astype(BF16)
+        grown[0].start()
+        n1[c, :rows] = times(gq, body, m1[c, :rows]).astype(BF16)
+        grown[1].start()
+        for one in grown:
+            one.wait_recv()
+        for j in range(2):
+            t0[pl.ds(j * wide, wide), :] = n0[j, :rows].T
+            t1[pl.ds(j * wide, wide), :] = n1[j, :rows].T
+        for one in grown + mate_q:
+            one.wait_send()
+        mate_g.wait_send()
+
+        @pl.when(even)
+        def _():
+            for one in side_q:
+                one.wait_send()
+            side_g.wait_send()
+
+    @pl.when(even & upper)
+    def _():
+        for one in pair_up:
+            one.wait_send()
+        pair_map.wait_send()
+
+    below = pieces((LA, LB), zy.at[c], zy.at[c], {"tm": tm - 2})
     beside = pieces((OA, OB), zy.at[c], zy.at[c], across)
     inner = pieces((FA, FB), zy.at[c], zy.at[c], mate)
 
@@ -283,9 +391,16 @@
         yin[...] = jnp.zeros_like(yin)
 
     def relay(n):
-        @pl.when(even)
+        @pl.when(even & upper)
         def _():
             chain[n].wait_recv()
+            below[n].start()
+            inner[n].start()
+            beside[n].start()
+
+        @pl.when(even & lower)
+        def _():
+            below[n].wait_recv()
             inner[n].start()
             beside[n].start()
 
@@ -300,8 +415,8 @@
         inner[0].wait_recv()
         unpack_first(zy, yin)
 
-    edges(0, 1.0, m0)
-    edges(1, -1.0, m1)
+    edges(0, 1.0, n0)
+    edges(1, -1.0, n1)
     for step in range(2):
         kb_edge = mm(cov, kb[step, c].astype(BF16))
         cross_ref[step] = kb_edge
@@ -321,24 +436,24 @@
             span = pl.ds(j * wide, wide)
             out_ref[step, span] = p[span] + mt(kb[step, j].astype(BF16), edge)
 
-    passes = even & (k > 0) & jnp.logical_not(last)
-    w = state(m0)
+    passes = heads & jnp.logical_not(last)
+    w = state(n0)
     pm0[mine] += mm(t0[mine, :], w)
 
     @pl.when(passes)
     def _():
-        pack_first(pm0, kb[0, c])
+        pack_first(zs, pm0, kb[0, c])
         chain[0].start()
 
     pm0[other] += mm(t0[other, :], w)
 
     @pl.when(passes)
     def _():
-        pack_second(pm0)
+        pack_second(zs, pm0)
         chain[1].start()
 
     emit(0, pm0)
-    w = state(m1)
+    w = state(n1)
     for j in range(2):
         span = pl.ds(j * wide, wide)
         pm1[span] += mm(t1[span, :], w)
@@ -357,7 +472,12 @@
         for one in beside:
             one.wait_send()
 
-    @pl.when(even & (k > 0))
+    @pl.when(takes)
+    def _():
+        for one in below:
+            one.wait_send()
+
+    @pl.when(heads)
     def _():
         for one in chain:
             one.wait_send()
@@ -396,6 +516,12 @@
             pltpu.VMEM((2, tall, wide), BF16),
             pltpu.VMEM((nodes, wide), F32),
             pltpu.VMEM((nodes, wide), F32),
+            pltpu.VMEM((2, packed, wide // 2), BF16),
+            pltpu.VMEM((packed, wide // 2), BF16),
+            pltpu.VMEM((2, nodes, wide), BF16),
+            pltpu.VMEM((tall, nodes), BF16),
+            pltpu.VMEM((2, tall, wide), BF16),
+            pltpu.VMEM((2, tall, wide), BF16),
             pltpu.VMEM((tall, nodes), BF16),
             pltpu.VMEM((count, 2, effects, wide), F32),
             pltpu.SemaphoreType.DMA((COPIES,)),

time: 49.9 us -> 46.5 us (0.932)
  Pallas kernels: 46.2 us -> 42.7 us
    pallas_call x1, Pallas kernels: 46.2 us -> 42.7 us  [shards(): pl.pallas_call(kernel, out_shape=(jax.ShapeDtypeStruct((count, nodes, wid...]
where the time goes in v5:
time: 46.5 us; the launch traced here: 46.3 us
  Pallas kernels  42.7 us (92%)
  local copies, waits for them, and re-layouts  2.93 us (6%)
  between operations  0.65 us (1%)
    pallas_call x1, Pallas kernels, shards(): pl.pallas_call(kernel, out_shape=(jax.ShapeDtypeStruct((count, nodes, wid...  42.7 us
    unnamed x4, local copies, waits for them, and re-layouts  2.93 us

profile of v5, /device:TPU:3, one launch (start us, length us, event | category | flops | bytes accessed | tf_op | source)
XLA Modules:
  0.0 46.3 jit_solution(14465952229417355138)
XLA Ops:
  0.6 42.7 %shard_map.59 = (f32[2,512,256]{2,1,0:T(8,128)}, f32[2,32,256]{2,1,0:T(8,128)}) custom-call(f32[2,512,256]{2,1,0:T(8,128)} %d_hbm.1, bf16[2,512,256]{2,1,0:T(8,128)(2,1)} %g_hbm.1, bf16[2,32,256]{2,1,0:T(8,128)(2,1)} %h_hbm.1, f32[32,32]{1,0:T(8,128)} %a_hbm.1), custom_call_target="tpu_custom_call" | custom-call | tf_op jit(solution)/shard_map/pallas_call | solution.py:492
  43.4 0.0 copy-start
  43.4 2.3 %copy.8 = f32[2,512,256]{2,1,0:T(8,128)} copy(f32[2,512,256]{2,1,0:T(8,128)} %get-tuple-element.4) | data formatting | bytes 2097152
  45.7 0.0 copy-done
  45.7 0.6 %copy.9 = f32[2,32,256]{2,1,0:T(8,128)} copy(f32[2,32,256]{2,1,0:T(8,128)S(1)} %copy-done) | data formatting | bytes 131072
Async XLA Ops:
  43.4 2.3 %copy-start = (f32[2,32,256]{2,1,0:T(8,128)S(1)}, f32[2,32,256]{2,1,0:T(8,128)}, u32[]{:S(2)}) copy-start(f32[2,32,256]{2,1,0:T(8,128)} %get-tuple-element.5) | copy-start | bytes 196612

commit v6 on v5

--- a/solution.py
+++ b/solution.py
@@ -9,8 +9,8 @@
 MESH = pl.DeviceIdType.MESH
 F32 = jnp.float32
 BF16 = jnp.bfloat16
-G0, G1, DH1, GC, XA, XB, XFA, XFB, XG, XGF, M1X, M0X, YA, YB, OA, OB, FA, FB, QA, QB, QG, QFA, QFB, QFG, QOA, QOB, QOG, N0, N1, LA, LB = range(31)
-COPIES = 31
+G0, G1, DH1, GC, XA, XB, XFA, XFB, XG, XGF, M1X, M0X, YA, YB, OA, OB, FA, FB, QA, QB, QG, QFA, QFB, QFG, QOA, QOB, QOG, N0, N1, LA, LB, QG2, QFG2, QOG2 = range(34)
+COPIES = 34
 
 
 def mm(left, right):
@@ -208,7 +208,12 @@
 
     chain = pieces((YA, YB), zs, zy.at[c], {"tm": tm - 2})
     pair_up = pieces((QA, QB), zt, zq.at[c], {"tm": tm - 2})
-    pair_map = copy(QG, m0.at[c, body], gq.at[c], {"tm": tm - 2})
+    parts = [pl.ds(0, wide), pl.ds(wide, wide)]
+
+    def halves(ids, src, device):
+        return [copy(i, src.at[c, r], gq.at[c, r], device) for i, r in zip(ids, parts)]
+
+    pair_map = halves((QG, QG2), m0, {"tm": tm - 2})
 
     @pl.when(odd)
     def _():
@@ -262,7 +267,8 @@
 
         @pl.when(upper)
         def _():
-            pair_map.start()
+            for one in pair_map:
+                one.start()
 
         m1[c, :rows] = times(g1cf, body, g1f[c]).astype(BF16)
         m1x = copy(M1X, m1.at[c], m1.at[c], mate)
@@ -291,8 +297,8 @@
 
     side_q = pieces((QOA, QOB), zq.at[c], zq.at[c], across)
     mate_q = pieces((QFA, QFB), zq.at[c], zq.at[c], mate)
-    side_g = copy(QOG, gq.at[c], gq.at[c], across)
-    mate_g = copy(QFG, gq.at[c], gq.at[c], mate)
+    side_g = halves((QOG, QOG2), gq, across)
+    mate_g = halves((QFG, QFG2), gq, mate)
     grown = [copy(N0, n0.at[c], n0.at[c], mate), copy(N1, n1.at[c], n1.at[c], mate)]
 
     @pl.when(lower)
@@ -341,16 +347,19 @@
 
         @pl.when(even)
         def _():
-            pair_map.wait_recv()
-            mate_g.start()
-            side_g.start()
+            for n in range(2):
+                pair_map[n].wait_recv()
+                side_g[n].start()
+                mate_g[n].start()
 
         @pl.when(odd)
         def _():
-            side_g.wait_recv()
-            mate_g.start()
-
-        mate_g.wait_recv()
+            for n in range(2):
+                side_g[n].wait_recv()
+                mate_g[n].start()
+
+        for one in mate_g:
+            one.wait_recv()
         n0[c, :rows] = times(gq, body, m0[c, :rows]).astype(BF16)
         grown[0].start()
         n1[c, :rows] = times(gq, body, m1[c, :rows]).astype(BF16)
@@ -362,19 +371,22 @@
             t1[pl.ds(j * wide, wide), :] = n1[j, :rows].T
         for one in grown + mate_q:
             one.wait_send()
-        mate_g.wait_send()
+        for one in mate_g:
+            one.wait_send()
 
         @pl.when(even)
         def _():
             for one in side_q:
                 one.wait_send()
-            side_g.wait_send()
+            for one in side_g:
+                one.wait_send()
 
     @pl.when(even & upper)
     def _():
         for one in pair_up:
             one.wait_send()
-        pair_map.wait_send()
+        for one in pair_map:
+            one.wait_send()
 
     below = pieces((LA, LB), zy.at[c], zy.at[c], {"tm": tm - 2})
     beside = pieces((OA, OB), zy.at[c], zy.at[c], across)

time: 46.5 us -> 44.8 us (0.963)
  Pallas kernels: 42.7 us -> 41.1 us
    pallas_call x1, Pallas kernels: 42.7 us -> 41.1 us  [shards(): pl.pallas_call(kernel, out_shape=(jax.ShapeDtypeStruct((count, nodes, wid...]
where the time goes in v6:
time: 44.8 us; the launch traced here: 44.6 us
  Pallas kernels  41.1 us (92%)
  local copies, waits for them, and re-layouts  2.93 us (7%)
  between operations  0.65 us (1%)
    pallas_call x1, Pallas kernels, shards(): pl.pallas_call(kernel, out_shape=(jax.ShapeDtypeStruct((count, nodes, wid...  41.1 us
    unnamed x4, local copies, waits for them, and re-layouts  2.93 us

profile of v6, /device:TPU:3, one launch (start us, length us, event | category | flops | bytes accessed | tf_op | source)
XLA Modules:
  0.0 44.6 jit_solution(8019811997607963291)
XLA Ops:
  0.6 41.1 %shard_map.59 = (f32[2,512,256]{2,1,0:T(8,128)}, f32[2,32,256]{2,1,0:T(8,128)}) custom-call(f32[2,512,256]{2,1,0:T(8,128)} %d_hbm.1, bf16[2,512,256]{2,1,0:T(8,128)(2,1)} %g_hbm.1, bf16[2,32,256]{2,1,0:T(8,128)(2,1)} %h_hbm.1, f32[32,32]{1,0:T(8,128)} %a_hbm.1), custom_call_target="tpu_custom_call" | custom-call | tf_op jit(solution)/shard_map/pallas_call | solution.py:504
  41.7 0.0 copy-start
  41.7 2.3 %copy.8 = f32[2,512,256]{2,1,0:T(8,128)} copy(f32[2,512,256]{2,1,0:T(8,128)} %get-tuple-element.4) | data formatting | bytes 2097152
  44.0 0.0 copy-done
  44.0 0.6 %copy.9 = f32[2,32,256]{2,1,0:T(8,128)} copy(f32[2,32,256]{2,1,0:T(8,128)S(1)} %copy-done) | data formatting | bytes 131072
Async XLA Ops:
  41.7 2.3 %copy-start = (f32[2,32,256]{2,1,0:T(8,128)S(1)}, f32[2,32,256]{2,1,0:T(8,128)}, u32[]{:S(2)}) copy-start(f32[2,32,256]{2,1,0:T(8,128)} %get-tuple-element.5) | copy-start | bytes 196612
